TPU v7x, 32 devices: a whole 2x2x4 slice. The times are simulated.
32 devices in a mesh: group: 4 (over y, x), owner: 8 (over z, core).
Axes of the slice: x: 2, y: 2, z: 4, core: 2. Of those that a mesh axis runs over, the one named last changes fastest.
Arguments:
- field: float32 [64, 4096], P(None, ('group', 'owner')), may hold values from -6 to 6
- contrast: float32 [64, 4096], P(None, ('group', 'owner')), may hold values from 0.1 to 2
- incident: float32 [64, 4096], P(None, ('group', 'owner')), may hold values from -6 to 6
- near_lists: int32 [27, 4096], P(None, ('group', 'owner')), may hold values from -1 to 128, as said below
- far_lists: int32 [316, 4672], P(None, ('group', 'owner')), may hold values from -1 to 128, as said below
- near_mats: float32 [27, 64, 64], replicated, may hold values from -0.15625 to 0.15625
- far_mats: float32 [316, 49, 49], replicated, may hold values from -0.0625 to 0.0625
- up_mats: float32 [8, 49, 49], replicated, may hold values from -0.3125 to 0.3125
- down_mats: float32 [8, 49, 49], replicated, may hold values from -0.875 to 0.875
- moment_map: float32 [49, 64], replicated, may hold values from -0.75 to 0.75
- local_map: float32 [64, 49], replicated, may hold values from -0.5 to 0.5
Outputs:
- new_field: float32 [64, 4096], P(None, ('group', 'owner'))
Inputs may be any that keep to these rules, and one draw needn't show every extreme that they name: -1 marks an empty slot; otherwise b + near_lists[k, b] - 64 is a leaf box, and slot 13 of every box holds 64. `far_lists`: -1 marks an empty slot; otherwise the entry names a box of the column's level as the steps say: below level 2 an entry of 0 to w_l, at level 2 any box of that level.
All inputs are finite; a program needn't handle non-finite values.
Results may differ from a plain program's by a relative error of at most 0.0003.
Values sent between devices are 32-bit elements; how exact they have to be, the bound alone decides.
No kernel may reach another device: no remote copies, remote signals or barrier semaphores. Data moves between devices by JAX's collectives and lax.ppermute only.
A program may use at most 128 MiB of HBM per device.

v0:
```python
import jax
import jax.numpy as jnp
from jax import lax
from jax.experimental import pallas as pl
from jax.experimental.pallas import tpu as pltpu
from jax.sharding import PartitionSpec as P

AXES = ("group", "owner")
HIGH = lax.Precision.HIGHEST
LANES = 128
GROUP = 7
VMEM = pl.BlockSpec(memory_space=pltpu.VMEM)
SMEM = pl.BlockSpec(memory_space=pltpu.SMEM)
NN = (((1,), (0,)), ((), ()))
NT = (((1,), (1,)), ((), ()))
GATHER = lax.GatherDimensionNumbers(
    offset_dims=(),
    collapsed_slice_dims=(1,),
    start_index_map=(1,),
    operand_batching_dims=(0,),
    start_indices_batching_dims=(0,),
)


def lane_gather(values, lanes):
    return lax.gather(
        values,
        lanes[..., None],
        GATHER,
        (1, 1),
        mode=lax.GatherScatterMode.PROMISE_IN_BOUNDS,
    )


def exact_dot(lhs, rhs, dims):
    return lax.dot_general(
        lhs, rhs, dims, precision=HIGH, preferred_element_type=jnp.float32
    )


def fast_dot(lhs, rhs, dims):
    return lax.dot_general(lhs, rhs, dims, preferred_element_type=jnp.float32)


def halves(value):
    upper = value.astype(jnp.bfloat16)
    lower = (value - upper.astype(jnp.float32)).astype(jnp.bfloat16)
    return upper, lower


def split_dot(lhs, rhs, dims):
    (lhs_hi, lhs_lo), (rhs_hi, rhs_lo) = lhs, rhs
    return (
        fast_dot(lhs_hi, rhs_hi, dims)
        + fast_dot(lhs_hi, rhs_lo, dims)
        + fast_dot(lhs_lo, rhs_hi, dims)
    )


def parents_of(children_ref, count, up_ref):
    terms = up_ref.shape[1]
    total = None
    for c in range(8):
        part = exact_dot(
            children_ref[pl.ds(c, count, stride=8), :],
            up_ref[pl.ds(c, terms, stride=8), :],
            NT,
        )
        total = part if total is None else total + part
    return total


def source_kernel(field_ref, contrast_ref, map_ref, up_ref, source_ref, tops_ref, low, mid):
    source = contrast_ref[...] * field_ref[...]
    source_ref[...] = source
    terms = map_ref.shape[0]
    low[...] = exact_dot(map_ref[...], source, NN).T
    mid[...] = parents_of(low, mid.shape[0], up_ref)
    tops = parents_of(mid, mid.shape[0] // 8, up_ref)
    devices = tops_ref.shape[0]
    tops_ref[...] = jnp.zeros(tops_ref.shape, jnp.float32)
    tops_ref[:, 0:terms] = jnp.broadcast_to(tops[0:1], (devices, terms))
    tops_ref[:, 64 : 64 + terms] = jnp.broadcast_to(tops[1:2], (devices, terms))


def local_kernel(
    source_ref,
    first_ref,
    second_ref,
    incident_ref,
    near_lists_ref,
    far_lists_ref,
    near_mats_ref,
    far_mats_ref,
    map_ref,
    up_ref,
    odd_ref,
    partial_ref,
    far_ref,
    rim,
    low_own,
    low_rim,
    low_rows,
    mid,
    mid_lanes,
    lane_at,
    kind_at,
    picked_hi,
    picked_lo,
):
    leaves = source_ref.shape[1]
    half = leaves // 2
    terms = map_ref.shape[0]
    mids = leaves // 8
    slots = far_mats_ref.shape[2]
    lane = lax.broadcasted_iota(jnp.int32, source_ref.shape, 1)
    odd = odd_ref[0]
    from_first = (lane // half) == odd
    rim[...] = jnp.where(from_first, first_ref[...], second_ref[...])
    own_low = exact_dot(map_ref[...], source_ref[...], NN)
    rim_low = exact_dot(map_ref[...], rim[...], NN)
    low_own[0:terms, :] = own_low
    low_rim[0:terms, :] = rim_low
    low_rows[0:leaves, :] = own_low.T
    low_rows[leaves : 2 * leaves, :] = rim_low.T
    mid[...] = parents_of(low_rows, 2 * mids, up_ref)
    mid_lanes[...] = jnp.zeros(mid_lanes.shape, jnp.float32)
    mid_lanes[0:terms, 0 : 2 * mids] = mid[...].T

    lane_at[...] = jnp.zeros(lane_at.shape, jnp.int32)
    kind_at[...] = jnp.zeros(kind_at.shape, jnp.int32)
    entry = far_lists_ref[0:leaves, :]
    at = lax.broadcasted_iota(jnp.int32, entry.shape, 0) + entry - half
    own = (at >= 0) & (at < leaves)
    lane_at[0:leaves, 0:slots] = at & (leaves - 1)
    kind_at[0:leaves, 0:slots] = jnp.where(entry < 0, 0, jnp.where(own, 1, 2))
    entry = far_lists_ref[leaves : leaves + mids, :]
    at = lax.broadcasted_iota(jnp.int32, entry.shape, 0) + entry - mids // 2
    own = (at >= 0) & (at < mids)
    lane_at[leaves : leaves + mids, 0:slots] = (at & (mids - 1)) + jnp.where(own, 0, mids)
    kind_at[leaves : leaves + mids, 0:slots] = jnp.where(entry < 0, 0, 1)

    near_lane = lax.broadcasted_iota(jnp.int32, (8, leaves), 1)
    cells = source_ref.shape[0]

    def near_step(k, total):
        entry = jnp.broadcast_to(near_lists_ref[pl.ds(k, 1), :], (8, leaves))
        at = near_lane + entry - half
        inside = (at >= 0) & (at < leaves)
        use_own = (entry >= 0) & inside
        use_rim = (entry >= 0) & jnp.logical_not(inside)
        lanes = at & (leaves - 1)
        rows = []
        for r in range(0, cells, 8):
            from_own = lane_gather(source_ref[r : r + 8, :], lanes)
            from_rim = lane_gather(rim[r : r + 8, :], lanes)
            rows.append(
                jnp.where(use_own, from_own, jnp.where(use_rim, from_rim, 0.0))
            )
        picked = halves(jnp.concatenate(rows, axis=0))
        return total + split_dot(halves(near_mats_ref[k]), picked, NN)

    partial_ref[...] = lax.fori_loop(
        0, near_lists_ref.shape[0], near_step, incident_ref[...], unroll=3
    )

    def far_step(g, total):
        for row in range(0, leaves + mids, 16):
            for column in range(0, lane_at.shape[1], LANES):
                lanes = lane_at[row : row + 16, column : column + LANES]
                kinds = kind_at[row : row + 16, column : column + LANES]
                use_own = kinds == 1
                use_rim = kinds == 2
                for u in range(GROUP):
                    t = g * GROUP + u
                    if row < leaves:
                        own_row = jnp.broadcast_to(low_own[pl.ds(t, 1), :], (16, LANES))
                        rim_row = jnp.broadcast_to(low_rim[pl.ds(t, 1), :], (16, LANES))
                        value = jnp.where(
                            use_own,
                            lane_gather(own_row, lanes),
                            jnp.where(use_rim, lane_gather(rim_row, lanes), 0.0),
                        )
                    else:
                        mid_row = jnp.broadcast_to(mid_lanes[pl.ds(t, 1), :], (16, LANES))
                        value = jnp.where(use_own, lane_gather(mid_row, lanes), 0.0)
                    upper, lower = halves(value)
                    picked_hi[u, row : row + 16, column : column + LANES] = upper
                    picked_lo[u, row : row + 16, column : column + LANES] = lower
        for u in range(GROUP):
            t = g * GROUP + u
            matrix = halves(far_mats_ref[:, pl.ds(t, 1), :][:, 0, :])
            picked = (picked_hi[u, :, 0:slots], picked_lo[u, :, 0:slots])
            total = total + split_dot(picked, matrix, NT)
        return total

    far_ref[...] = lax.fori_loop(
        0, terms // GROUP, far_step, jnp.zeros(far_ref.shape, jnp.float32)
    )


def final_kernel(
    every_top_ref,
    far_lists_ref,
    far_mats_ref,
    far_ref,
    partial_ref,
    down_ref,
    local_ref,
    out_ref,
    top_lanes,
    sums,
    tops,
    mid,
    low,
):
    devices = every_top_ref.shape[0]
    terms = far_ref.shape[1]
    leaves = partial_ref.shape[1]
    mids = leaves // 8
    count = far_lists_ref.shape[0] - leaves - mids
    slots = far_mats_ref.shape[2]
    every = every_top_ref[...]
    both = jnp.concatenate([every[:, 0:64], every[:, 64:128]], axis=0)
    tiles = top_lanes.shape[0]
    wide = tiles * LANES
    if wide > both.shape[0]:
        both = jnp.concatenate(
            [both, jnp.zeros((wide - both.shape[0], both.shape[1]), jnp.float32)], axis=0
        )
    for tile in range(tiles):
        top_lanes[tile] = both[tile * LANES : (tile + 1) * LANES].T
    rows = top_lanes.shape[1] // 8
    picked = []
    for j in range(count):
        entry = far_lists_ref[pl.ds(leaves + mids + j, 1), :]
        code = jnp.where(entry < 0, -1, (entry & 1) * devices + (entry >> 1))
        columns = []
        for column in range(0, slots, LANES):
            width = min(LANES, slots - column)
            part = code[:, column : column + width]
            if width < LANES:
                part = jnp.concatenate(
                    [part, jnp.full((1, LANES - width), -1, jnp.int32)], axis=1
                )
            part = jnp.broadcast_to(part, (56, LANES))
            value = jnp.zeros((56, LANES), jnp.float32)
            for tile in range(tiles):
                here = (part >> 7) == tile
                value = jnp.where(
                    here, lane_gather(top_lanes[tile, 0:56, :], part & (LANES - 1)), value
                )
            columns.append(value)
        picked.append(jnp.concatenate(columns, axis=1)[0:terms, 0:slots])

    def top_step(s, carry):
        matrix = far_mats_ref[s]
        for j in range(count):
            sums[j, pl.ds(s, 1), :] = jnp.sum(matrix * picked[j], axis=0, keepdims=True)
        return carry

    lax.fori_loop(0, terms, top_step, 0, unroll=7)
    ones = jnp.ones((8, slots), jnp.float32)
    for j in range(count):
        tops[pl.ds(j, 1), :] = exact_dot(ones, sums[j], NT)[0:1]
    top_rows = tops[...]
    for c in range(8):
        matrix = down_ref[pl.ds(c, terms, stride=8), :]
        part = exact_dot(top_rows, matrix, NT)
        mid[pl.ds(c, count, stride=8), :] = part[0:count]
    mid_rows = mid[...] + far_ref[leaves : leaves + mids, :]
    for c in range(8):
        matrix = down_ref[pl.ds(c, terms, stride=8), :]
        low[pl.ds(c, mids, stride=8), :] = exact_dot(mid_rows, matrix, NT)
    low_rows = low[...] + far_ref[0:leaves, :]
    out_ref[...] = partial_ref[...] + exact_dot(local_ref[...].T, low_rows, NT)


def body(
    field,
    contrast,
    incident,
    near_lists,
    far_lists,
    near_mats,
    far_mats,
    up_mats,
    down_mats,
    moment_map,
    local_map,
):
    devices = lax.axis_size(AXES)
    rank = lax.axis_index(AXES)
    cells, leaves = field.shape
    terms = moment_map.shape[0]
    mids = leaves // 8
    slots = far_mats.shape[0]
    assert leaves == LANES and terms % GROUP == 0 and far_lists.shape[1] == 146
    up_rows = up_mats.transpose(1, 0, 2).reshape(8 * terms, terms)
    down_rows = down_mats.transpose(1, 0, 2).reshape(8 * terms, terms)
    far_cube = far_mats.transpose(1, 2, 0)
    far_rows = far_lists.T
    wide = -(-slots // LANES) * LANES
    f32 = jnp.float32

    source, own_tops = pl.pallas_call(
        source_kernel,
        out_shape=(
            jax.ShapeDtypeStruct((cells, leaves), f32),
            jax.ShapeDtypeStruct((devices, LANES), f32),
        ),
        in_specs=[VMEM] * 4,
        out_specs=(VMEM, VMEM),
        scratch_shapes=[pltpu.VMEM((leaves, terms), f32), pltpu.VMEM((mids, terms), f32)],
    )(field, contrast, moment_map, up_rows)

    pairs = [(i, i ^ 1) for i in range(devices)]
    shifted = [(0, 0), (devices - 1, devices - 1)]
    for i in range(1, devices - 1, 2):
        shifted += [(i, i + 1), (i + 1, i)]
    first = lax.ppermute(source, AXES, pairs)
    second = lax.ppermute(source, AXES, shifted)
    every_top = lax.all_to_all(own_tops, AXES, split_axis=0, concat_axis=0, tiled=True)

    odd = jnp.reshape(rank % 2, (1,)).astype(jnp.int32)
    partial, far_sums = pl.pallas_call(
        local_kernel,
        out_shape=(
            jax.ShapeDtypeStruct((cells, leaves), f32),
            jax.ShapeDtypeStruct((leaves + mids, terms), f32),
        ),
        in_specs=[VMEM] * 10 + [SMEM],
        out_specs=(VMEM, VMEM),
        scratch_shapes=[
            pltpu.VMEM((cells, leaves), f32),
            pltpu.VMEM((56, leaves), f32),
            pltpu.VMEM((56, leaves), f32),
            pltpu.VMEM((2 * leaves, terms), f32),
            pltpu.VMEM((2 * mids, terms), f32),
            pltpu.VMEM((56, LANES), f32),
            pltpu.VMEM((leaves + mids, wide), jnp.int32),
            pltpu.VMEM((leaves + mids, wide), jnp.int32),
            pltpu.VMEM((GROUP, leaves + mids, wide), jnp.bfloat16),
            pltpu.VMEM((GROUP, leaves + mids, wide), jnp.bfloat16),
        ],
        compiler_params=pltpu.CompilerParams(vmem_limit_bytes=40 << 20),
    )(
        source,
        first,
        second,
        incident,
        near_lists,
        far_rows,
        near_mats,
        far_cube,
        moment_map,
        up_rows,
        odd,
    )

    tiles = -(-2 * devices // LANES)
    return pl.pallas_call(
        final_kernel,
        out_shape=jax.ShapeDtypeStruct((cells, leaves), f32),
        in_specs=[VMEM] * 7,
        out_specs=VMEM,
        scratch_shapes=[
            pltpu.VMEM((tiles, 64, LANES), f32),
            pltpu.VMEM((2, terms, slots), f32),
            pltpu.VMEM((8, terms), f32),
            pltpu.VMEM((mids, terms), f32),
            pltpu.VMEM((leaves, terms), f32),
        ],
        compiler_params=pltpu.CompilerParams(vmem_limit_bytes=40 << 20),
    )(every_top, far_rows, far_cube, far_sums, partial, down_rows, local_map.T)


def solution(mesh):
    columns = P(None, AXES)
    in_specs = (columns,) * 5 + (P(),) * 6
    return jax.shard_map(body, mesh=mesh, in_specs=in_specs, out_specs=columns, check_vma=False)
```

profile of v0, /device:TPU:0, one launch (start us, length us, event | category | flops | bytes accessed | tf_op | source)
XLA Modules:
  0.0 52.9 jit_solution(1958045969330106379)
XLA Ops:
  0.0 0.0 copy-start.3
  0.0 0.0 copy-start.10
  0.0 3.6 %shard_map.109 = (f32[64,128]{1,0:T(8,128)}, f32[32,128]{1,0:T(8,128)}) custom-call(f32[64,128]{1,0:T(8,128)} %field_ref.1, f32[64,128]{1,0:T(8,128)} %contrast_ref.1, f32[49,64]{1,0:T(8,128)} %map_ref.3, f32[392,49]{1,0:T(8,128)} %bitcast.18), custom_call_target="tpu_custom_call" | custom-call | tf_op jit(solution)/shard_map/pallas_call | solution.py:306
  3.6 1.4 %collective-permute-start.1 = (f32[64,128]{1,0:T(8,128)}, f32[64,128]{1,0:T(8,128)S(1)}, u32[]{:S(2)}, u32[]{:S(2)}) collective-permute-start(f32[64,128]{1,0:T(8,128)} %get-tuple-element.10.source_ref), channel_id=1, source_target_pairs={{0,0},{31,31},{1,2},{2,1},{3,4},{4,3},{5,6},{6,5},{7,8},{8,7},{9,1... | collective-permute-start | bytes 98312 | tf_op jit(solution)/shard_map/ppermute | solution.py:322
  5.0 3.7 %collective-permute-start = (f32[64,128]{1,0:T(8,128)}, f32[64,128]{1,0:T(8,128)S(1)}, u32[]{:S(2)}, u32[]{:S(2)}) collective-permute-start(f32[64,128]{1,0:T(8,128)} %get-tuple-element.10.source_ref), channel_id=1, source_target_pairs={{0,1},{1,0},{2,3},{3,2},{4,5},{5,4},{6,7},{7,6},{8,9},{9,8},{10,11... | collective-permute-start | bytes 98312 | tf_op jit(solution)/shard_map/ppermute | solution.py:321
  8.8 4.8 %all-to-all-start = ((f32[32,1,128]{2,1,0:T(1,128)}), f32[32,1,128]{2,1,0:T(1,128)S(1)}, u32[]{:S(2)}, u32[]{:S(2)}) async-start(f32[32,1,128]{2,1,0:T(1,128)} %bitcast.23), calls=%async_computation | async-start | bytes 32768 | tf_op jit(solution)/shard_map/all_to_all | solution.py:323
  13.6 0.0 collective-permute-done.1.second_ref
  13.6 0.0 collective-permute-done.first_ref
  13.6 0.0 copy-start
  13.6 2.2 %copy-done = f32[316,49,49]{0,2,1:T(8,128)S(1)} copy-done((f32[316,49,49]{0,2,1:T(8,128)S(1)}, f32[316,49,49]{0,2,1:T(8,128)}, u32[]{:S(2)}) %copy-start) | copy-done | bytes 3034888
  15.8 0.0 copy-start.2
  15.8 0.9 %copy-done.2 = s32[316,146]{0,1:T(8,128)S(1)} copy-done((s32[316,146]{0,1:T(8,128)S(1)}, s32[316,146]{0,1:T(8,128)}, u32[]{:S(2)}) %copy-start.2) | copy-done | bytes 184568
  16.8 0.0 copy-start.4
  16.8 1.2 %copy-done.4 = f32[27,64,64]{2,1,0:T(8,128)S(1)} copy-done((f32[27,64,64]{2,1,0:T(8,128)S(1)}, f32[27,64,64]{2,1,0:T(8,128)}, u32[]{:S(2)}) %copy-start.4) | copy-done | bytes 442392
  17.9 0.0 copy-start.5
  17.9 0.9 %copy-done.5 = f32[8,49,49]{2,0,1:T(8,128)S(1)} copy-done((f32[8,49,49]{2,0,1:T(8,128)S(1)}, f32[8,49,49]{2,0,1:T(8,128)}, u32[]{:S(2)}) %copy-start.5) | copy-done | bytes 76856
  18.9 0.0 copy-start.7
  18.9 0.7 %copy-done.7 = f32[49,64]{1,0:T(8,128)S(1)} copy-done((f32[49,64]{1,0:T(8,128)S(1)}, f32[49,64]{1,0:T(8,128)}, u32[]{:S(2)}) %copy-start.7) | copy-done | bytes 12568
  19.6 0.0 copy-start.8
  19.6 0.8 %copy-done.8 = f32[64,128]{1,0:T(8,128)S(1)} copy-done((f32[64,128]{1,0:T(8,128)S(1)}, f32[64,128]{1,0:T(8,128)}, u32[]{:S(2)}) %copy-start.8) | copy-done | bytes 32792
  20.4 0.8 %copy-done.9 = f32[64,128]{1,0:T(8,128)S(1)} copy-done((f32[64,128]{1,0:T(8,128)S(1)}, f32[64,128]{1,0:T(8,128)}, u32[]{:S(2)}) %copy-start.9) | copy-done | bytes 32792
  21.1 0.0 copy-start.11
  21.1 0.7 %copy-done.11 = s32[27,128]{1,0:T(8,128)S(1)} copy-done((s32[27,128]{1,0:T(8,128)S(1)}, s32[27,128]{1,0:T(8,128)}, u32[]{:S(2)}) %copy-start.11) | copy-done | bytes 13848
  21.9 0.0 copy-start.6
  21.9 25.3 %shard_map.110 = (f32[64,128]{1,0:T(8,128)S(1)}, f32[144,49]{1,0:T(8,128)S(1)}) custom-call(f32[64,128]{1,0:T(8,128)S(1)} %copy-done.9, f32[64,128]{1,0:T(8,128)S(1)} %collective-permute-done.first_ref, f32[64,128]{1,0:T(8,128)S(1)} %collective-permute-done.1.second_ref, f32[64,128]{1,0:T(8,128)S(1)} %copy-done.8, s32[27,128]{1,0:T(8,128)S(1)} %copy-done.11, ...), custom_call_target="tpu_custom_call" | custom-call | tf_op jit(solution)/shard_map/pallas_call | solution.py:326
  47.1 0.0 all-to-all-done
  47.1 0.0 copy-done.3
  47.1 0.0 copy-done.10
  47.1 0.0 copy-done.6
  47.2 0.0 copy-start.1
  47.2 2.2 %copy-done.1 = f32[316,49,49]{0,2,1:T(8,128)S(1)} copy-done((f32[316,49,49]{0,2,1:T(8,128)S(1)}, f32[316,49,49]{0,2,1:T(8,128)}, u32[]{:S(2)}) %copy-start.1) | copy-done | bytes 3034888
  49.4 3.5 %shard_map.111 = f32[64,128]{1,0:T(8,128)} custom-call(f32[32,128]{1,0:T(8,128)S(1)} %bitcast.21, s32[146,316]{1,0:T(8,128)S(1)} %bitcast.17, f32[49,49,316]{2,1,0:T(8,128)S(1)} %bitcast.15, f32[144,49]{1,0:T(8,128)S(1)} %get-tuple-element.11.far_ref, f32[64,128]{1,0:T(8,128)S(1)} %get-tuple-element.12.partial_ref, f32[392,49]{1,0:T(8,128)S(1)} %bitcast.20, ...), custom_call_target="tpu_custom_call" | custom-call | tf_op jit(solution)/shard_map/pallas_call | solution.py:362
  (1 shorter events, 0.0 us)
Async XLA Ops:
  0.0 47.1 %copy-start.3 = (s32[316,146]{0,1:T(8,128)S(1)}, s32[316,146]{0,1:T(8,128)}, u32[]{:S(2)}) copy-start(s32[316,146]{0,1:T(8,128)} %param.15) | copy-start | bytes 553636
  0.0 47.1 %copy-start.10 = (f32[64,49]{0,1:T(8,128)S(1)}, f32[64,49]{0,1:T(8,128)}, u32[]{:S(2)}) copy-start(f32[64,49]{0,1:T(8,128)} %param.21) | copy-start | bytes 37636
  3.6 10.0 %collective-permute-start.1 = (f32[64,128]{1,0:T(8,128)}, f32[64,128]{1,0:T(8,128)S(1)}, u32[]{:S(2)}, u32[]{:S(2)}) collective-permute-start(f32[64,128]{1,0:T(8,128)} %get-tuple-element.10.source_ref), channel_id=1, source_target_pairs={{0,0},{31,31},{1,2},{2,1},{3,4},{4,3},{5,6},{6,5},{7,8},{8,7},{9,1... | collective-permute-start | bytes 98312 | tf_op jit(solution)/shard_map/ppermute | solution.py:322
  5.0 8.6 %collective-permute-start = (f32[64,128]{1,0:T(8,128)}, f32[64,128]{1,0:T(8,128)S(1)}, u32[]{:S(2)}, u32[]{:S(2)}) collective-permute-start(f32[64,128]{1,0:T(8,128)} %get-tuple-element.10.source_ref), channel_id=1, source_target_pairs={{0,1},{1,0},{2,3},{3,2},{4,5},{5,4},{6,7},{7,6},{8,9},{9,8},{10,11... | collective-permute-start | bytes 98312 | tf_op jit(solution)/shard_map/ppermute | solution.py:321
  8.8 38.4 %all-to-all-start = ((f32[32,1,128]{2,1,0:T(1,128)}), f32[32,1,128]{2,1,0:T(1,128)S(1)}, u32[]{:S(2)}, u32[]{:S(2)}) async-start(f32[32,1,128]{2,1,0:T(1,128)} %bitcast.23), calls=%async_computation | async-start | bytes 32768 | tf_op jit(solution)/shard_map/all_to_all | solution.py:323
  13.6 2.2 %copy-start = (f32[316,49,49]{0,2,1:T(8,128)S(1)}, f32[316,49,49]{0,2,1:T(8,128)}, u32[]{:S(2)}) copy-start(f32[316,49,49]{0,2,1:T(8,128)} %param.17) | copy-start | bytes 9104596
  15.8 0.9 %copy-start.2 = (s32[316,146]{0,1:T(8,128)S(1)}, s32[316,146]{0,1:T(8,128)}, u32[]{:S(2)}) copy-start(s32[316,146]{0,1:T(8,128)} %param.15) | copy-start | bytes 553636
  16.8 1.2 %copy-start.4 = (f32[27,64,64]{2,1,0:T(8,128)S(1)}, f32[27,64,64]{2,1,0:T(8,128)}, u32[]{:S(2)}) copy-start(f32[27,64,64]{2,1,0:T(8,128)} %near_mats_ref.1) | copy-start | bytes 1327108
  17.9 0.9 %copy-start.5 = (f32[8,49,49]{2,0,1:T(8,128)S(1)}, f32[8,49,49]{2,0,1:T(8,128)}, u32[]{:S(2)}) copy-start(f32[8,49,49]{2,0,1:T(8,128)} %param.18) | copy-start | bytes 230500
  18.9 0.7 %copy-start.7 = (f32[49,64]{1,0:T(8,128)S(1)}, f32[49,64]{1,0:T(8,128)}, u32[]{:S(2)}) copy-start(f32[49,64]{1,0:T(8,128)} %map_ref.3) | copy-start | bytes 37636
  19.6 0.8 %copy-start.8 = (f32[64,128]{1,0:T(8,128)S(1)}, f32[64,128]{1,0:T(8,128)}, u32[]{:S(2)}) copy-start(f32[64,128]{1,0:T(8,128)} %incident_ref.1) | copy-start | bytes 98308
  20.4 0.8 %copy-start.9 = (f32[64,128]{1,0:T(8,128)S(1)}, f32[64,128]{1,0:T(8,128)}, u32[]{:S(2)}) copy-start(f32[64,128]{1,0:T(8,128)} %get-tuple-element.10.source_ref) | copy-start | bytes 98308
  21.1 0.7 %copy-start.11 = (s32[27,128]{1,0:T(8,128)S(1)}, s32[27,128]{1,0:T(8,128)}, u32[]{:S(2)}) copy-start(s32[27,128]{1,0:T(8,128)} %near_lists_ref.1) | copy-start | bytes 41476
  21.9 25.3 %copy-start.6 = (f32[8,49,49]{2,0,1:T(8,128)S(1)}, f32[8,49,49]{2,0,1:T(8,128)}, u32[]{:S(2)}) copy-start(f32[8,49,49]{2,0,1:T(8,128)} %param.19) | copy-start | bytes 230500
  47.2 2.2 %copy-start.1 = (f32[316,49,49]{0,2,1:T(8,128)S(1)}, f32[316,49,49]{0,2,1:T(8,128)}, u32[]{:S(2)}) copy-start(f32[316,49,49]{0,2,1:T(8,128)} %param.17) | copy-start | bytes 9104596
where the time goes:
time: 53.5 us; the launch traced here: 52.9 us
  Pallas kernels  32.4 us (61%)
  local copies, waits for them, and re-layouts  10.4 us (19%)
  starting transfers between devices  9.97 us (19%)
    pallas_call x1, Pallas kernels, body(): pl.pallas_call(local_kernel, out_shape=(jax.ShapeDtypeStruct((cells, leav...  25.3 us
    unnamed x24, local copies, waits for them, and re-layouts  10.4 us
    all_to_all x1, starting transfers between devices, body(): lax.all_to_all(own_tops, AXES, split_axis=0, concat_axis=0, tiled=True)  4.84 us
    ppermute x1, starting transfers between devices, body(): first = lax.ppermute(source, AXES, pairs)  3.73 us
    pallas_call x1, Pallas kernels, body(): pl.pallas_call(source_kernel, out_shape=(jax.ShapeDtypeStruct((cells, lea...  3.61 us
    pallas_call x1, Pallas kernels, body(): pl.pallas_call(final_kernel, out_shape=jax.ShapeDtypeStruct((cells, leave...  3.53 us
    ppermute x1, starting transfers between devices, body(): second = lax.ppermute(source, AXES, shifted)  1.41 us
  transfers between devices with their start and end apart: 3, of which 0 were waited for; matrix products, arithmetic and copies ran while one was open for 0% of the time, Pallas kernels for 48%

commit v1 on v0

--- a/solution.py
+++ b/solution.py
@@ -8,9 +8,10 @@
 AXES = ("group", "owner")
 HIGH = lax.Precision.HIGHEST
 LANES = 128
-GROUP = 7
+GROUP = 8
 VMEM = pl.BlockSpec(memory_space=pltpu.VMEM)
 SMEM = pl.BlockSpec(memory_space=pltpu.SMEM)
+HBM = pl.BlockSpec(memory_space=pltpu.HBM)
 NN = (((1,), (0,)), ((), ()))
 NT = (((1,), (1,)), ((), ()))
 GATHER = lax.GatherDimensionNumbers(
@@ -83,20 +84,35 @@
     tops_ref[:, 64 : 64 + terms] = jnp.broadcast_to(tops[1:2], (devices, terms))
 
 
+def split_block(value):
+    upper, lower = halves(value)
+    return jnp.concatenate([upper, lower], axis=0)
+
+
 def local_kernel(
+    odd_ref,
+    source_hbm,
+    first_hbm,
+    second_hbm,
+    incident_hbm,
+    near_lists_hbm,
+    far_lists_hbm,
+    near_mats_hbm,
+    far_mats_hbm,
+    map_hbm,
+    up_hbm,
+    partial_ref,
+    far_ref,
     source_ref,
     first_ref,
     second_ref,
-    incident_ref,
-    near_lists_ref,
-    far_lists_ref,
-    near_mats_ref,
-    far_mats_ref,
-    map_ref,
-    up_ref,
-    odd_ref,
-    partial_ref,
-    far_ref,
+    incident,
+    near_lists,
+    far_lists,
+    near_mats,
+    far_mats,
+    map_mat,
+    up_mat,
     rim,
     low_own,
     low_rim,
@@ -107,44 +123,74 @@
     kind_at,
     picked_hi,
     picked_lo,
+    matrices,
+    spread,
+    sems,
 ):
-    leaves = source_ref.shape[1]
+    moves = [
+        pltpu.make_async_copy(src, dst, sems.at[i])
+        for i, (src, dst) in enumerate(
+            [
+                (map_hbm, map_mat),
+                (source_hbm, source_ref),
+                (first_hbm, first_ref),
+                (second_hbm, second_ref),
+                (up_hbm, up_mat),
+                (far_lists_hbm, far_lists),
+                (near_lists_hbm, near_lists),
+                (near_mats_hbm, near_mats),
+                (incident_hbm, incident),
+                (far_mats_hbm, far_mats),
+            ]
+        )
+    ]
+    for move in moves:
+        move.start()
+    cells, leaves = source_ref.shape
     half = leaves // 2
-    terms = map_ref.shape[0]
+    terms = map_mat.shape[0]
     mids = leaves // 8
-    slots = far_mats_ref.shape[2]
+    targets = leaves + mids
+    slots = far_mats.shape[2]
+    wide = lane_at.shape[1]
+    lane_at[...] = jnp.zeros(lane_at.shape, jnp.int16)
+    kind_at[...] = jnp.zeros(kind_at.shape, jnp.int16)
+    mid_lanes[...] = jnp.zeros(mid_lanes.shape, jnp.float32)
     lane = lax.broadcasted_iota(jnp.int32, source_ref.shape, 1)
-    odd = odd_ref[0]
-    from_first = (lane // half) == odd
+    from_first = (lane // half) == odd_ref[0]
+    for move in moves[0:4]:
+        move.wait()
     rim[...] = jnp.where(from_first, first_ref[...], second_ref[...])
-    own_low = exact_dot(map_ref[...], source_ref[...], NN)
-    rim_low = exact_dot(map_ref[...], rim[...], NN)
+
+    own_low = exact_dot(map_mat[...], source_ref[...], NN)
+    rim_low = exact_dot(map_mat[...], rim[...], NN)
     low_own[0:terms, :] = own_low
     low_rim[0:terms, :] = rim_low
     low_rows[0:leaves, :] = own_low.T
     low_rows[leaves : 2 * leaves, :] = rim_low.T
-    mid[...] = parents_of(low_rows, 2 * mids, up_ref)
-    mid_lanes[...] = jnp.zeros(mid_lanes.shape, jnp.float32)
+    moves[4].wait()
+    mid[...] = parents_of(low_rows, 2 * mids, up_mat)
     mid_lanes[0:terms, 0 : 2 * mids] = mid[...].T
 
-    lane_at[...] = jnp.zeros(lane_at.shape, jnp.int32)
-    kind_at[...] = jnp.zeros(kind_at.shape, jnp.int32)
-    entry = far_lists_ref[0:leaves, :]
+    moves[5].wait()
+    entry = far_lists[0:leaves, :]
     at = lax.broadcasted_iota(jnp.int32, entry.shape, 0) + entry - half
     own = (at >= 0) & (at < leaves)
-    lane_at[0:leaves, 0:slots] = at & (leaves - 1)
-    kind_at[0:leaves, 0:slots] = jnp.where(entry < 0, 0, jnp.where(own, 1, 2))
-    entry = far_lists_ref[leaves : leaves + mids, :]
+    lane_at[0:leaves, 0:slots] = (at & (leaves - 1)).astype(jnp.int16)
+    kind_at[0:leaves, 0:slots] = jnp.where(entry < 0, 0, jnp.where(own, 1, 2)).astype(jnp.int16)
+    entry = far_lists[leaves:targets, :]
     at = lax.broadcasted_iota(jnp.int32, entry.shape, 0) + entry - mids // 2
     own = (at >= 0) & (at < mids)
-    lane_at[leaves : leaves + mids, 0:slots] = (at & (mids - 1)) + jnp.where(own, 0, mids)
-    kind_at[leaves : leaves + mids, 0:slots] = jnp.where(entry < 0, 0, 1)
-
+    lanes = (at & (mids - 1)) + jnp.where(own, 0, mids)
+    lane_at[leaves:targets, 0:slots] = lanes.astype(jnp.int16)
+    kind_at[leaves:targets, 0:slots] = jnp.where(entry < 0, 0, 1).astype(jnp.int16)
+
+    for move in moves[6:9]:
+        move.wait()
     near_lane = lax.broadcasted_iota(jnp.int32, (8, leaves), 1)
-    cells = source_ref.shape[0]
 
     def near_step(k, total):
-        entry = jnp.broadcast_to(near_lists_ref[pl.ds(k, 1), :], (8, leaves))
+        entry = jnp.broadcast_to(near_lists[pl.ds(k, 1), :], (8, leaves))
         at = near_lane + entry - half
         inside = (at >= 0) & (at < leaves)
         use_own = (entry >= 0) & inside
@@ -158,48 +204,75 @@
                 jnp.where(use_own, from_own, jnp.where(use_rim, from_rim, 0.0))
             )
         picked = halves(jnp.concatenate(rows, axis=0))
-        return total + split_dot(halves(near_mats_ref[k]), picked, NN)
+        return total + split_dot(halves(near_mats[k]), picked, NN)
 
     partial_ref[...] = lax.fori_loop(
-        0, near_lists_ref.shape[0], near_step, incident_ref[...], unroll=3
+        0, near_lists.shape[0], near_step, incident[...], unroll=9
     )
 
-    def far_step(g, total):
-        for row in range(0, leaves + mids, 16):
-            for column in range(0, lane_at.shape[1], LANES):
+    moves[9].wait()
+    padding = jnp.zeros((terms, wide - slots), jnp.float32)
+    rest = jnp.zeros((64 - terms, wide), jnp.float32)
+
+    def far_block(first, count, cube, total):
+        for u in range(count):
+            for i, table in enumerate((low_own, low_rim, mid_lanes)):
+                row = jnp.broadcast_to(table[pl.ds(first + u, 1), :], (16, LANES))
+                spread[6 * u + 2 * i], spread[6 * u + 2 * i + 1] = halves(row)
+            matrix = jnp.concatenate([cube[u], padding], axis=1)
+            matrix = jnp.concatenate([matrix, rest], axis=0)
+            upper, lower = halves(matrix)
+            matrices[0:64, u * wide : (u + 1) * wide] = upper
+            matrices[64:128, u * wide : (u + 1) * wide] = lower
+        nothing = jnp.zeros((16, LANES), jnp.bfloat16)
+        for row in range(0, targets, 16):
+            for column in range(0, wide, LANES):
                 lanes = lane_at[row : row + 16, column : column + LANES]
                 kinds = kind_at[row : row + 16, column : column + LANES]
                 use_own = kinds == 1
                 use_rim = kinds == 2
-                for u in range(GROUP):
-                    t = g * GROUP + u
-                    if row < leaves:
-                        own_row = jnp.broadcast_to(low_own[pl.ds(t, 1), :], (16, LANES))
-                        rim_row = jnp.broadcast_to(low_rim[pl.ds(t, 1), :], (16, LANES))
-                        value = jnp.where(
-                            use_own,
-                            lane_gather(own_row, lanes),
-                            jnp.where(use_rim, lane_gather(rim_row, lanes), 0.0),
-                        )
-                    else:
-                        mid_row = jnp.broadcast_to(mid_lanes[pl.ds(t, 1), :], (16, LANES))
-                        value = jnp.where(use_own, lane_gather(mid_row, lanes), 0.0)
-                    upper, lower = halves(value)
-                    picked_hi[u, row : row + 16, column : column + LANES] = upper
-                    picked_lo[u, row : row + 16, column : column + LANES] = lower
-        for u in range(GROUP):
-            t = g * GROUP + u
-            matrix = halves(far_mats_ref[:, pl.ds(t, 1), :][:, 0, :])
-            picked = (picked_hi[u, :, 0:slots], picked_lo[u, :, 0:slots])
-            total = total + split_dot(picked, matrix, NT)
-        return total
-
-    far_ref[...] = lax.fori_loop(
-        0, terms // GROUP, far_step, jnp.zeros(far_ref.shape, jnp.float32)
-    )
+                for u in range(count):
+                    place = u * wide + column
+                    for i, picked in enumerate((picked_hi, picked_lo)):
+                        if row < leaves:
+                            value = jnp.where(
+                                use_own,
+                                lane_gather(spread[6 * u + i], lanes),
+                                jnp.where(
+                                    use_rim, lane_gather(spread[6 * u + 2 + i], lanes), nothing
+                                ),
+                            )
+                        else:
+                            value = jnp.where(
+                                use_own, lane_gather(spread[6 * u + 4 + i], lanes), nothing
+                            )
+                        picked[row : row + 16, place : place + LANES] = value
+        depth = count * wide
+        both = fast_dot(picked_hi[:, 0:depth], matrices[:, 0:depth], NT)
+        small = fast_dot(picked_lo[:, 0:depth], matrices[0:64, 0:depth], NT)
+        return total + (both[:, 0:64] + both[:, 64:128] + small)
+
+    def far_step(g, total):
+        first = pl.multiple_of(g * GROUP, GROUP)
+        cube = jnp.swapaxes(far_mats[:, pl.ds(first, GROUP), :], 0, 1)
+        return far_block(first, GROUP, cube, total)
+
+    whole = terms // GROUP
+    total = lax.fori_loop(0, whole, far_step, jnp.zeros((targets, 64), jnp.float32))
+    for t in range(whole * GROUP, terms):
+        total = far_block(t, 1, far_mats[:, t, :][None], total)
+    far_ref[...] = total[:, 0:terms]
 
 
 def final_kernel(
+    every_top_hbm,
+    far_lists_hbm,
+    far_mats_hbm,
+    far_hbm,
+    partial_hbm,
+    down_hbm,
+    local_hbm,
+    out_ref,
     every_top_ref,
     far_lists_ref,
     far_mats_ref,
@@ -207,19 +280,41 @@
     partial_ref,
     down_ref,
     local_ref,
-    out_ref,
+    sems,
     top_lanes,
     sums,
     tops,
     mid,
     low,
 ):
+    blocks = 7
+    deep = far_mats_ref.shape[0] // blocks
+    pairs = [
+        (every_top_hbm, every_top_ref),
+        (far_lists_hbm, far_lists_ref),
+    ]
+    for i in range(blocks):
+        part = pl.ds(i * deep, deep)
+        pairs.append((far_mats_hbm.at[part], far_mats_ref.at[part]))
+    pairs += [
+        (far_hbm, far_ref),
+        (partial_hbm, partial_ref),
+        (down_hbm, down_ref),
+        (local_hbm, local_ref),
+    ]
+    moves = [
+        pltpu.make_async_copy(src, dst, sems.at[i]) for i, (src, dst) in enumerate(pairs)
+    ]
+    for move in moves:
+        move.start()
     devices = every_top_ref.shape[0]
     terms = far_ref.shape[1]
     leaves = partial_ref.shape[1]
     mids = leaves // 8
     count = far_lists_ref.shape[0] - leaves - mids
     slots = far_mats_ref.shape[2]
+    moves[0].wait()
+    moves[1].wait()
     every = every_top_ref[...]
     both = jnp.concatenate([every[:, 0:64], every[:, 64:128]], axis=0)
     tiles = top_lanes.shape[0]
@@ -253,13 +348,17 @@
             columns.append(value)
         picked.append(jnp.concatenate(columns, axis=1)[0:terms, 0:slots])
 
-    def top_step(s, carry):
+    def top_step(s):
         matrix = far_mats_ref[s]
         for j in range(count):
             sums[j, pl.ds(s, 1), :] = jnp.sum(matrix * picked[j], axis=0, keepdims=True)
-        return carry
-
-    lax.fori_loop(0, terms, top_step, 0, unroll=7)
+
+    for i in range(blocks):
+        moves[2 + i].wait()
+        for s in range(i * deep, (i + 1) * deep):
+            top_step(s)
+    for move in moves[2 + blocks :]:
+        move.wait()
     ones = jnp.ones((8, slots), jnp.float32)
     for j in range(count):
         tops[pl.ds(j, 1), :] = exact_dot(ones, sums[j], NT)[0:1]
@@ -295,7 +394,7 @@
     terms = moment_map.shape[0]
     mids = leaves // 8
     slots = far_mats.shape[0]
-    assert leaves == LANES and terms % GROUP == 0 and far_lists.shape[1] == 146
+    assert leaves == LANES and far_lists.shape[1] == 146
     up_rows = up_mats.transpose(1, 0, 2).reshape(8 * terms, terms)
     down_rows = down_mats.transpose(1, 0, 2).reshape(8 * terms, terms)
     far_cube = far_mats.transpose(1, 2, 0)
@@ -323,28 +422,43 @@
     every_top = lax.all_to_all(own_tops, AXES, split_axis=0, concat_axis=0, tiled=True)
 
     odd = jnp.reshape(rank % 2, (1,)).astype(jnp.int32)
+    targets = leaves + mids
+    near = near_lists.shape[0]
     partial, far_sums = pl.pallas_call(
         local_kernel,
         out_shape=(
             jax.ShapeDtypeStruct((cells, leaves), f32),
-            jax.ShapeDtypeStruct((leaves + mids, terms), f32),
+            jax.ShapeDtypeStruct((targets, terms), f32),
         ),
-        in_specs=[VMEM] * 10 + [SMEM],
+        in_specs=[SMEM] + [HBM] * 10,
         out_specs=(VMEM, VMEM),
         scratch_shapes=[
+            pltpu.VMEM((cells, leaves), f32),
+            pltpu.VMEM((cells, leaves), f32),
+            pltpu.VMEM((cells, leaves), f32),
+            pltpu.VMEM((cells, leaves), f32),
+            pltpu.VMEM((near, leaves), jnp.int32),
+            pltpu.VMEM(far_rows.shape, jnp.int32),
+            pltpu.VMEM((near, cells, cells), f32),
+            pltpu.VMEM((terms, terms, slots), f32),
+            pltpu.VMEM((terms, cells), f32),
+            pltpu.VMEM((8 * terms, terms), f32),
             pltpu.VMEM((cells, leaves), f32),
             pltpu.VMEM((56, leaves), f32),
             pltpu.VMEM((56, leaves), f32),
             pltpu.VMEM((2 * leaves, terms), f32),
             pltpu.VMEM((2 * mids, terms), f32),
             pltpu.VMEM((56, LANES), f32),
-            pltpu.VMEM((leaves + mids, wide), jnp.int32),
-            pltpu.VMEM((leaves + mids, wide), jnp.int32),
-            pltpu.VMEM((GROUP, leaves + mids, wide), jnp.bfloat16),
-            pltpu.VMEM((GROUP, leaves + mids, wide), jnp.bfloat16),
+            pltpu.VMEM((targets, wide), jnp.int16),
+            pltpu.VMEM((targets, wide), jnp.int16),
+            pltpu.VMEM((targets, GROUP * wide), jnp.bfloat16),
+            pltpu.VMEM((targets, GROUP * wide), jnp.bfloat16),
+            pltpu.VMEM((128, GROUP * wide), jnp.bfloat16),
+            pltpu.VMEM((6 * GROUP, 16, LANES), jnp.bfloat16),
+            pltpu.SemaphoreType.DMA((10,)),
         ],
-        compiler_params=pltpu.CompilerParams(vmem_limit_bytes=40 << 20),
     )(
+        odd,
         source,
         first,
         second,
@@ -355,23 +469,29 @@
         far_cube,
         moment_map,
         up_rows,
-        odd,
     )
 
     tiles = -(-2 * devices // LANES)
     return pl.pallas_call(
         final_kernel,
         out_shape=jax.ShapeDtypeStruct((cells, leaves), f32),
-        in_specs=[VMEM] * 7,
+        in_specs=[HBM] * 7,
         out_specs=VMEM,
         scratch_shapes=[
+            pltpu.VMEM((devices, LANES), f32),
+            pltpu.VMEM(far_rows.shape, jnp.int32),
+            pltpu.VMEM((terms, terms, slots), f32),
+            pltpu.VMEM((targets, terms), f32),
+            pltpu.VMEM((cells, leaves), f32),
+            pltpu.VMEM((8 * terms, terms), f32),
+            pltpu.VMEM((terms, cells), f32),
+            pltpu.SemaphoreType.DMA((13,)),
             pltpu.VMEM((tiles, 64, LANES), f32),
             pltpu.VMEM((2, terms, slots), f32),
             pltpu.VMEM((8, terms), f32),
             pltpu.VMEM((mids, terms), f32),
             pltpu.VMEM((leaves, terms), f32),
         ],
-        compiler_params=pltpu.CompilerParams(vmem_limit_bytes=40 << 20),
     )(every_top, far_rows, far_cube, far_sums, partial, down_rows, local_map.T)
 
 

time: 53.5 us -> 34.9 us (0.65)
  local copies, waits for them, and re-layouts: 10.4 us -> 1.19 us
  Pallas kernels: 32.4 us -> 23.4 us
    pallas_call x1, Pallas kernels: 25.3 us -> 15.2 us  [body(): pl.pallas_call(local_kernel, out_shape=(jax.ShapeDtypeStruct((cells, leav...]
    unnamed x24 -> x6, local copies, waits for them, and re-layouts: 10.4 us -> 1.19 us
    pallas_call x1, Pallas kernels: 3.53 us -> 4.65 us  [body(): pl.pallas_call(final_kernel, out_shape=jax.ShapeDtypeStruct((cells, leave...]
  transfers between devices with their start and end apart: 3 -> 3, of which waited for: 0 -> 0; matrix products, arithmetic and copies ran while one was open for 0% -> 0% of each run, Pallas kernels for 48% -> 44%
where the time goes in v1:
time: 34.9 us; the launch traced here: 34.6 us
  Pallas kernels  23.4 us (67%)
  starting transfers between devices  9.97 us (29%)
  local copies, waits for them, and re-layouts  1.19 us (3%)
    pallas_call x1, Pallas kernels, body(): pl.pallas_call(local_kernel, out_shape=(jax.ShapeDtypeStruct((cells, leav...  15.2 us
    all_to_all x1, starting transfers between devices, body(): lax.all_to_all(own_tops, AXES, split_axis=0, concat_axis=0, tiled=True)  4.84 us
    pallas_call x1, Pallas kernels, body(): pl.pallas_call(final_kernel, out_shape=jax.ShapeDtypeStruct((cells, leave...  4.65 us
    ppermute x1, starting transfers between devices, body(): first = lax.ppermute(source, AXES, pairs)  3.73 us
    pallas_call x1, Pallas kernels, body(): pl.pallas_call(source_kernel, out_shape=(jax.ShapeDtypeStruct((cells, lea...  3.57 us
    ppermute x1, starting transfers between devices, body(): second = lax.ppermute(source, AXES, shifted)  1.41 us
    unnamed x6, local copies, waits for them, and re-layouts  1.19 us
  transfers between devices with their start and end apart: 3, of which 0 were waited for; matrix products, arithmetic and copies ran while one was open for 0% of the time, Pallas kernels for 44%

profile of v1, /device:TPU:0, one launch (start us, length us, event | category | flops | bytes accessed | tf_op | source)
XLA Modules:
  0.0 34.6 jit_solution(6624549290606891486)
XLA Ops:
  0.0 3.6 %shard_map.109 = (f32[64,128]{1,0:T(8,128)}, f32[32,128]{1,0:T(8,128)}) custom-call(f32[64,128]{1,0:T(8,128)} %field_ref.1, f32[64,128]{1,0:T(8,128)} %contrast_ref.1, f32[49,64]{1,0:T(8,128)} %map_hbm.1, f32[392,49]{1,0:T(8,128)} %bitcast.18), custom_call_target="tpu_custom_call" | custom-call | tf_op jit(solution)/shard_map/pallas_call | solution.py:405
  3.6 1.4 %collective-permute-start.1 = (f32[64,128]{1,0:T(8,128)}, f32[64,128]{1,0:T(8,128)S(1)}, u32[]{:S(2)}, u32[]{:S(2)}) collective-permute-start(f32[64,128]{1,0:T(8,128)} %get-tuple-element.10.source_hbm), channel_id=1, source_target_pairs={{0,0},{31,31},{1,2},{2,1},{3,4},{4,3},{5,6},{6,5},{7,8},{8,7},{9,1... | collective-permute-start | bytes 98312 | tf_op jit(solution)/shard_map/ppermute | solution.py:421
  5.0 3.7 %collective-permute-start = (f32[64,128]{1,0:T(8,128)}, f32[64,128]{1,0:T(8,128)S(1)}, u32[]{:S(2)}, u32[]{:S(2)}) collective-permute-start(f32[64,128]{1,0:T(8,128)} %get-tuple-element.10.source_hbm), channel_id=1, source_target_pairs={{0,1},{1,0},{2,3},{3,2},{4,5},{5,4},{6,7},{7,6},{8,9},{9,8},{10,11... | collective-permute-start | bytes 98312 | tf_op jit(solution)/shard_map/ppermute | solution.py:420
  8.7 4.8 %all-to-all-start = ((f32[32,1,128]{2,1,0:T(1,128)}), f32[32,1,128]{2,1,0:T(1,128)S(1)}, u32[]{:S(2)}, u32[]{:S(2)}) async-start(f32[32,1,128]{2,1,0:T(1,128)} %bitcast.23), calls=%async_computation | async-start | bytes 32768 | tf_op jit(solution)/shard_map/all_to_all | solution.py:422
  13.6 0.0 collective-permute-done.1.second_hbm
  13.6 0.0 copy-start.1
  13.6 0.0 collective-permute-done.first_hbm
  13.6 0.0 copy-start.2
  13.6 0.6 %copy-done.1 = f32[64,128]{1,0:T(8,128)} copy-done((f32[64,128]{1,0:T(8,128)}, f32[64,128]{1,0:T(8,128)S(1)}, u32[]{:S(2)}) %copy-start.1) | copy-done | bytes 32792
  14.2 0.0 copy-done.2
  14.2 15.2 %shard_map.110 = (f32[64,128]{1,0:T(8,128)}, f32[144,49]{1,0:T(8,128)}) custom-call(s32[1]{0:T(128)} %bitcast.7.odd_ref, f32[64,128]{1,0:T(8,128)} %get-tuple-element.10.source_hbm, f32[64,128]{1,0:T(8,128)} %copy-done.2, f32[64,128]{1,0:T(8,128)} %copy-done.1, f32[64,128]{1,0:T(8,128)} %incident_hbm.1, s32[27,128]{1,0:T(8,128)} %near_lists_hbm.1, ...), custom_call_target="tpu_custom_call" | custom-call | tf_op jit(solution)/shard_map/pallas_call | solution.py:427
  29.4 0.0 all-to-all-done
  29.4 0.0 copy-start
  29.4 0.6 %copy-done = f32[32,1,128]{2,1,0:T(1,128)} copy-done((f32[32,1,128]{2,1,0:T(1,128)}, f32[32,1,128]{2,1,0:T(1,128)S(1)}, u32[]{:S(2)}) %copy-start) | copy-done | bytes 16408
  30.0 4.6 %shard_map.111 = f32[64,128]{1,0:T(8,128)} custom-call(f32[32,128]{1,0:T(8,128)} %bitcast.21, s32[146,316]{1,0:T(8,128)} %bitcast.17, f32[49,49,316]{2,1,0:T(8,128)} %bitcast.15, f32[144,49]{1,0:T(8,128)} %get-tuple-element.11.far_hbm, f32[64,128]{1,0:T(8,128)} %get-tuple-element.12.partial_hbm, f32[392,49]{1,0:T(8,128)} %bitcast.20, f32[49,64]{1,0:T(8,128)} %bitcast.22), custom_call_target="tpu_custom_call" | custom-call | tf_op jit(solution)/shard_map/pallas_call | solution.py:475
Async XLA Ops:
  3.6 10.0 %collective-permute-start.1 = (f32[64,128]{1,0:T(8,128)}, f32[64,128]{1,0:T(8,128)S(1)}, u32[]{:S(2)}, u32[]{:S(2)}) collective-permute-start(f32[64,128]{1,0:T(8,128)} %get-tuple-element.10.source_hbm), channel_id=1, source_target_pairs={{0,0},{31,31},{1,2},{2,1},{3,4},{4,3},{5,6},{6,5},{7,8},{8,7},{9,1... | collective-permute-start | bytes 98312 | tf_op jit(solution)/shard_map/ppermute | solution.py:421
  5.0 8.6 %collective-permute-start = (f32[64,128]{1,0:T(8,128)}, f32[64,128]{1,0:T(8,128)S(1)}, u32[]{:S(2)}, u32[]{:S(2)}) collective-permute-start(f32[64,128]{1,0:T(8,128)} %get-tuple-element.10.source_hbm), channel_id=1, source_target_pairs={{0,1},{1,0},{2,3},{3,2},{4,5},{5,4},{6,7},{7,6},{8,9},{9,8},{10,11... | collective-permute-start | bytes 98312 | tf_op jit(solution)/shard_map/ppermute | solution.py:420
  8.7 20.7 %all-to-all-start = ((f32[32,1,128]{2,1,0:T(1,128)}), f32[32,1,128]{2,1,0:T(1,128)S(1)}, u32[]{:S(2)}, u32[]{:S(2)}) async-start(f32[32,1,128]{2,1,0:T(1,128)} %bitcast.23), calls=%async_computation | async-start | bytes 32768 | tf_op jit(solution)/shard_map/all_to_all | solution.py:422
  13.6 0.6 %copy-start.1 = (f32[64,128]{1,0:T(8,128)}, f32[64,128]{1,0:T(8,128)S(1)}, u32[]{:S(2)}) copy-start(f32[64,128]{1,0:T(8,128)S(1)} %collective-permute-done.1.second_hbm) | copy-start | bytes 98308
  13.6 0.6 %copy-start.2 = (f32[64,128]{1,0:T(8,128)}, f32[64,128]{1,0:T(8,128)S(1)}, u32[]{:S(2)}) copy-start(f32[64,128]{1,0:T(8,128)S(1)} %collective-permute-done.first_hbm) | copy-start | bytes 98308
  29.4 0.6 %copy-start = (f32[32,1,128]{2,1,0:T(1,128)}, f32[32,1,128]{2,1,0:T(1,128)S(1)}, u32[]{:S(2)}) copy-start(f32[32,1,128]{2,1,0:T(1,128)S(1)} %all-to-all-done) | copy-start | bytes 49156

commit v2 on v1

--- a/solution.py
+++ b/solution.py
@@ -84,9 +84,12 @@
     tops_ref[:, 64 : 64 + terms] = jnp.broadcast_to(tops[1:2], (devices, terms))
 
 
-def split_block(value):
-    upper, lower = halves(value)
-    return jnp.concatenate([upper, lower], axis=0)
+def levels_of(columns):
+    most = jnp.max(jnp.abs(columns), axis=0, keepdims=True)
+    some = most > 1e-33
+    inverse = jnp.where(some, 32767.0 / jnp.where(some, most, 1.0), 0.0)
+    levels = jnp.floor(columns * inverse + 0.5).astype(jnp.int32)
+    return levels, most * (1.0 / 32767.0)
 
 
 def local_kernel(
@@ -120,11 +123,15 @@
     mid,
     mid_lanes,
     lane_at,
+    scale_at,
+    picked_a,
+    picked_b,
+    matrices_a,
+    matrices_b,
+    spread,
+    total,
+    steps,
     kind_at,
-    picked_hi,
-    picked_lo,
-    matrices,
-    spread,
     sems,
 ):
     moves = [
@@ -152,10 +159,11 @@
     mids = leaves // 8
     targets = leaves + mids
     slots = far_mats.shape[2]
-    wide = lane_at.shape[1]
+    tiles = lane_at.shape[0]
+    wide = tiles * LANES
     lane_at[...] = jnp.zeros(lane_at.shape, jnp.int16)
-    kind_at[...] = jnp.zeros(kind_at.shape, jnp.int16)
-    mid_lanes[...] = jnp.zeros(mid_lanes.shape, jnp.float32)
+    scale_at[...] = jnp.zeros(scale_at.shape, jnp.float32)
+    mid_lanes[...] = jnp.zeros(mid_lanes.shape, jnp.int32)
     lane = lax.broadcasted_iota(jnp.int32, source_ref.shape, 1)
     from_first = (lane // half) == odd_ref[0]
     for move in moves[0:4]:
@@ -164,31 +172,50 @@
 
     own_low = exact_dot(map_mat[...], source_ref[...], NN)
     rim_low = exact_dot(map_mat[...], rim[...], NN)
-    low_own[0:terms, :] = own_low
-    low_rim[0:terms, :] = rim_low
+    own_levels, own_step = levels_of(own_low)
+    rim_levels, rim_step = levels_of(rim_low)
+    low_own[0:terms, :] = own_levels
+    low_rim[0:terms, :] = -rim_levels
     low_rows[0:leaves, :] = own_low.T
     low_rows[leaves : 2 * leaves, :] = rim_low.T
     moves[4].wait()
     mid[...] = parents_of(low_rows, 2 * mids, up_mat)
-    mid_lanes[0:terms, 0 : 2 * mids] = mid[...].T
+    mid_levels, mid_step = levels_of(mid[...].T)
+    mid_lanes[0:terms, 0 : 2 * mids] = mid_levels
+    steps[...] = jnp.zeros(steps.shape, jnp.float32)
+    steps[0:1, :] = own_step
+    steps[1:2, :] = -rim_step
+    steps[2:3, 0 : 2 * mids] = mid_step
 
     moves[5].wait()
-    entry = far_lists[0:leaves, :]
-    at = lax.broadcasted_iota(jnp.int32, entry.shape, 0) + entry - half
-    own = (at >= 0) & (at < leaves)
-    lane_at[0:leaves, 0:slots] = (at & (leaves - 1)).astype(jnp.int16)
-    kind_at[0:leaves, 0:slots] = jnp.where(entry < 0, 0, jnp.where(own, 1, 2)).astype(jnp.int16)
-    entry = far_lists[leaves:targets, :]
-    at = lax.broadcasted_iota(jnp.int32, entry.shape, 0) + entry - mids // 2
-    own = (at >= 0) & (at < mids)
-    lanes = (at & (mids - 1)) + jnp.where(own, 0, mids)
-    lane_at[leaves:targets, 0:slots] = lanes.astype(jnp.int16)
-    kind_at[leaves:targets, 0:slots] = jnp.where(entry < 0, 0, 1).astype(jnp.int16)
+    near_lane = lax.broadcasted_iota(jnp.int32, (8, leaves), 1)
+    for i in range(tiles):
+        width = min(LANES, slots - i * LANES)
+        entry = far_lists[0:targets, i * LANES : i * LANES + width]
+        row = lax.broadcasted_iota(jnp.int32, entry.shape, 0)
+        leaf = row < leaves
+        at = entry + jnp.where(leaf, row - half, row - leaves - mids // 2)
+        own = (at >= 0) & (at < jnp.where(leaf, leaves, mids))
+        lanes = jnp.where(leaf, at & (leaves - 1), (at & (mids - 1)) + jnp.where(own, 0, mids))
+        lane_at[i, :, 0:width] = lanes.astype(jnp.int16)
+        kind_at[:, 0:width] = jnp.where(entry < 0, 0, jnp.where(own | (row >= leaves), 1, 2))
+        for first in range(0, targets, 8):
+            part = slice(first, first + 8)
+            at = lane_at[i, part, :].astype(jnp.int32)
+            kinds = kind_at[part, :]
+            if width < LANES:
+                kinds = jnp.where(near_lane < width, kinds, 0)
+            if first < leaves:
+                own = lane_gather(jnp.broadcast_to(steps[0:1, :], (8, LANES)), at)
+                rim_step = lane_gather(jnp.broadcast_to(steps[1:2, :], (8, LANES)), at)
+                step = jnp.where(kinds == 1, own, jnp.where(kinds == 2, rim_step, 0.0))
+            else:
+                step = lane_gather(jnp.broadcast_to(steps[2:3, :], (8, LANES)), at)
+                step = jnp.where(kinds == 1, step, 0.0)
+            scale_at[i, part, :] = step
 
     for move in moves[6:9]:
         move.wait()
-    near_lane = lax.broadcasted_iota(jnp.int32, (8, leaves), 1)
-
     def near_step(k, total):
         entry = jnp.broadcast_to(near_lists[pl.ds(k, 1), :], (8, leaves))
         at = near_lane + entry - half
@@ -213,55 +240,71 @@
     moves[9].wait()
     padding = jnp.zeros((terms, wide - slots), jnp.float32)
     rest = jnp.zeros((64 - terms, wide), jnp.float32)
-
-    def far_block(first, count, cube, total):
+    total[...] = jnp.zeros(total.shape, jnp.float32)
+
+    def fill(first, count, cube, picked, matrices):
         for u in range(count):
             for i, table in enumerate((low_own, low_rim, mid_lanes)):
                 row = jnp.broadcast_to(table[pl.ds(first + u, 1), :], (16, LANES))
-                spread[6 * u + 2 * i], spread[6 * u + 2 * i + 1] = halves(row)
+                spread[3 * u + i] = row.astype(jnp.int16)
             matrix = jnp.concatenate([cube[u], padding], axis=1)
             matrix = jnp.concatenate([matrix, rest], axis=0)
             upper, lower = halves(matrix)
-            matrices[0:64, u * wide : (u + 1) * wide] = upper
-            matrices[64:128, u * wide : (u + 1) * wide] = lower
-        nothing = jnp.zeros((16, LANES), jnp.bfloat16)
+            for i in range(tiles):
+                piece = slice(i * LANES, (i + 1) * LANES)
+                matrices[u * tiles + i, 0:64, :] = upper[:, piece]
+                matrices[u * tiles + i, 64:128, :] = lower[:, piece]
         for row in range(0, targets, 16):
-            for column in range(0, wide, LANES):
-                lanes = lane_at[row : row + 16, column : column + LANES]
-                kinds = kind_at[row : row + 16, column : column + LANES]
-                use_own = kinds == 1
-                use_rim = kinds == 2
+            for tile in range(tiles):
+                lanes = lane_at[tile, row : row + 16, :]
+                scale = scale_at[tile, row : row + 16, :]
+                use_own = scale > 0.0
                 for u in range(count):
-                    place = u * wide + column
-                    for i, picked in enumerate((picked_hi, picked_lo)):
-                        if row < leaves:
-                            value = jnp.where(
-                                use_own,
-                                lane_gather(spread[6 * u + i], lanes),
-                                jnp.where(
-                                    use_rim, lane_gather(spread[6 * u + 2 + i], lanes), nothing
-                                ),
-                            )
-                        else:
-                            value = jnp.where(
-                                use_own, lane_gather(spread[6 * u + 4 + i], lanes), nothing
-                            )
-                        picked[row : row + 16, place : place + LANES] = value
-        depth = count * wide
-        both = fast_dot(picked_hi[:, 0:depth], matrices[:, 0:depth], NT)
-        small = fast_dot(picked_lo[:, 0:depth], matrices[0:64, 0:depth], NT)
-        return total + (both[:, 0:64] + both[:, 64:128] + small)
-
-    def far_step(g, total):
+                    if row < leaves:
+                        value = jnp.where(
+                            use_own,
+                            lane_gather(spread[3 * u], lanes).astype(jnp.int32),
+                            lane_gather(spread[3 * u + 1], lanes).astype(jnp.int32),
+                        )
+                    else:
+                        value = lane_gather(spread[3 * u + 2], lanes).astype(jnp.int32)
+                    upper, lower = halves(value.astype(jnp.float32) * scale)
+                    picked[u * tiles + tile, row : row + 16, :] = upper
+                    picked[u * tiles + tile, targets + row : targets + row + 16, :] = lower
+
+    def add(count, picked, matrices):
+        every = range(count * tiles)
+        left = jnp.concatenate([picked[i] for i in every], axis=1)
+        right = jnp.concatenate([matrices[i] for i in every], axis=1)
+        total[...] += fast_dot(left, right, NT)
+
+    def fill_block(g, picked, matrices):
         first = pl.multiple_of(g * GROUP, GROUP)
         cube = jnp.swapaxes(far_mats[:, pl.ds(first, GROUP), :], 0, 1)
-        return far_block(first, GROUP, cube, total)
+        fill(first, GROUP, cube, picked, matrices)
 
     whole = terms // GROUP
-    total = lax.fori_loop(0, whole, far_step, jnp.zeros((targets, 64), jnp.float32))
+    rounds = (whole - 1) // 2
+    fill_block(0, picked_a, matrices_a)
+
+    def two_blocks(i, carry):
+        fill_block(2 * i + 1, picked_b, matrices_b)
+        add(GROUP, picked_a, matrices_a)
+        fill_block(2 * i + 2, picked_a, matrices_a)
+        add(GROUP, picked_b, matrices_b)
+        return carry
+
+    lax.fori_loop(0, rounds, two_blocks, 0)
+    buffers = [(picked_a, matrices_a), (picked_b, matrices_b)]
+    for g in range(2 * rounds + 1, whole):
+        fill_block(g, *buffers[g % 2])
+        add(GROUP, *buffers[(g - 1) % 2])
+    add(GROUP, *buffers[(whole - 1) % 2])
     for t in range(whole * GROUP, terms):
-        total = far_block(t, 1, far_mats[:, t, :][None], total)
-    far_ref[...] = total[:, 0:terms]
+        fill(t, 1, far_mats[:, t, :][None], *buffers[whole % 2])
+        add(1, *buffers[whole % 2])
+    sums = total[0:targets, :] + total[targets : 2 * targets, :]
+    far_ref[...] = sums[:, 0:terms] + sums[:, 64 : 64 + terms]
 
 
 def final_kernel(
@@ -444,17 +487,21 @@
             pltpu.VMEM((terms, cells), f32),
             pltpu.VMEM((8 * terms, terms), f32),
             pltpu.VMEM((cells, leaves), f32),
-            pltpu.VMEM((56, leaves), f32),
-            pltpu.VMEM((56, leaves), f32),
+            pltpu.VMEM((56, leaves), jnp.int32),
+            pltpu.VMEM((56, leaves), jnp.int32),
             pltpu.VMEM((2 * leaves, terms), f32),
             pltpu.VMEM((2 * mids, terms), f32),
-            pltpu.VMEM((56, LANES), f32),
-            pltpu.VMEM((targets, wide), jnp.int16),
-            pltpu.VMEM((targets, wide), jnp.int16),
-            pltpu.VMEM((targets, GROUP * wide), jnp.bfloat16),
-            pltpu.VMEM((targets, GROUP * wide), jnp.bfloat16),
-            pltpu.VMEM((128, GROUP * wide), jnp.bfloat16),
-            pltpu.VMEM((6 * GROUP, 16, LANES), jnp.bfloat16),
+            pltpu.VMEM((56, LANES), jnp.int32),
+            pltpu.VMEM((wide // LANES, targets, LANES), jnp.int16),
+            pltpu.VMEM((wide // LANES, targets, LANES), f32),
+            pltpu.VMEM((GROUP * wide // LANES, 2 * targets, LANES), jnp.bfloat16),
+            pltpu.VMEM((GROUP * wide // LANES, 2 * targets, LANES), jnp.bfloat16),
+            pltpu.VMEM((GROUP * wide // LANES, 128, LANES), jnp.bfloat16),
+            pltpu.VMEM((GROUP * wide // LANES, 128, LANES), jnp.bfloat16),
+            pltpu.VMEM((3 * GROUP, 16, LANES), jnp.int16),
+            pltpu.VMEM((2 * targets, LANES), f32),
+            pltpu.VMEM((8, LANES), f32),
+            pltpu.VMEM((targets, LANES), jnp.int32),
             pltpu.SemaphoreType.DMA((10,)),
         ],
     )(

time: 34.9 us -> 29.7 us (0.85)
  Pallas kernels: 23.4 us -> 18.2 us
    pallas_call x1, Pallas kernels: 15.2 us -> 9.95 us  [body(): pl.pallas_call(local_kernel, out_shape=(jax.ShapeDtypeStruct((cells, leav...]
  transfers between devices with their start and end apart: 3 -> 3, of which waited for: 0 -> 0; matrix products, arithmetic and copies ran while one was open for 0% -> 0% of each run, Pallas kernels for 44% -> 34%
where the time goes in v2:
time: 29.7 us; the launch traced here: 29.4 us
  Pallas kernels  18.2 us (61%)
  starting transfers between devices  9.97 us (34%)
  local copies, waits for them, and re-layouts  1.19 us (4%)
    pallas_call x1, Pallas kernels, body(): pl.pallas_call(local_kernel, out_shape=(jax.ShapeDtypeStruct((cells, leav...  9.95 us
    all_to_all x1, starting transfers between devices, body(): lax.all_to_all(own_tops, AXES, split_axis=0, concat_axis=0, tiled=True)  4.84 us
    pallas_call x1, Pallas kernels, body(): pl.pallas_call(final_kernel, out_shape=jax.ShapeDtypeStruct((cells, leave...  4.65 us
    ppermute x1, starting transfers between devices, body(): first = lax.ppermute(source, AXES, pairs)  3.73 us
    pallas_call x1, Pallas kernels, body(): pl.pallas_call(source_kernel, out_shape=(jax.ShapeDtypeStruct((cells, lea...  3.57 us
    ppermute x1, starting transfers between devices, body(): second = lax.ppermute(source, AXES, shifted)  1.41 us
    unnamed x6, local copies, waits for them, and re-layouts  1.19 us
  transfers between devices with their start and end apart: 3, of which 0 were waited for; matrix products, arithmetic and copies ran while one was open for 0% of the time, Pallas kernels for 34%

profile of v2, /device:TPU:0, one launch (start us, length us, event | category | flops | bytes accessed | tf_op | source)
XLA Modules:
  0.0 29.4 jit_solution(12511438545366845362)
XLA Ops:
  0.0 3.6 %shard_map.109 = (f32[64,128]{1,0:T(8,128)}, f32[32,128]{1,0:T(8,128)}) custom-call(f32[64,128]{1,0:T(8,128)} %field_ref.1, f32[64,128]{1,0:T(8,128)} %contrast_ref.1, f32[49,64]{1,0:T(8,128)} %map_hbm.1, f32[392,49]{1,0:T(8,128)} %bitcast.18), custom_call_target="tpu_custom_call" | custom-call | tf_op jit(solution)/shard_map/pallas_call | solution.py:448
  3.6 1.4 %collective-permute-start.1 = (f32[64,128]{1,0:T(8,128)}, f32[64,128]{1,0:T(8,128)S(1)}, u32[]{:S(2)}, u32[]{:S(2)}) collective-permute-start(f32[64,128]{1,0:T(8,128)} %get-tuple-element.10.source_hbm), channel_id=1, source_target_pairs={{0,0},{31,31},{1,2},{2,1},{3,4},{4,3},{5,6},{6,5},{7,8},{8,7},{9,1... | collective-permute-start | bytes 98312 | tf_op jit(solution)/shard_map/ppermute | solution.py:464
  5.0 3.7 %collective-permute-start = (f32[64,128]{1,0:T(8,128)}, f32[64,128]{1,0:T(8,128)S(1)}, u32[]{:S(2)}, u32[]{:S(2)}) collective-permute-start(f32[64,128]{1,0:T(8,128)} %get-tuple-element.10.source_hbm), channel_id=1, source_target_pairs={{0,1},{1,0},{2,3},{3,2},{4,5},{5,4},{6,7},{7,6},{8,9},{9,8},{10,11... | collective-permute-start | bytes 98312 | tf_op jit(solution)/shard_map/ppermute | solution.py:463
  8.7 4.8 %all-to-all-start = ((f32[32,1,128]{2,1,0:T(1,128)}), f32[32,1,128]{2,1,0:T(1,128)S(1)}, u32[]{:S(2)}, u32[]{:S(2)}) async-start(f32[32,1,128]{2,1,0:T(1,128)} %bitcast.23), calls=%async_computation | async-start | bytes 32768 | tf_op jit(solution)/shard_map/all_to_all | solution.py:465
  13.6 0.0 collective-permute-done.1.second_hbm
  13.6 0.0 copy-start.1
  13.6 0.0 collective-permute-done.first_hbm
  13.6 0.0 copy-start.2
  13.6 0.6 %copy-done.1 = f32[64,128]{1,0:T(8,128)} copy-done((f32[64,128]{1,0:T(8,128)}, f32[64,128]{1,0:T(8,128)S(1)}, u32[]{:S(2)}) %copy-start.1) | copy-done | bytes 32792
  14.2 0.0 copy-done.2
  14.2 10.0 %shard_map.110 = (f32[64,128]{1,0:T(8,128)}, f32[144,49]{1,0:T(8,128)}) custom-call(s32[1]{0:T(128)} %bitcast.7.odd_ref, f32[64,128]{1,0:T(8,128)} %get-tuple-element.10.source_hbm, f32[64,128]{1,0:T(8,128)} %copy-done.2, f32[64,128]{1,0:T(8,128)} %copy-done.1, f32[64,128]{1,0:T(8,128)} %incident_hbm.1, s32[27,128]{1,0:T(8,128)} %near_lists_hbm.1, ...), custom_call_target="tpu_custom_call" | custom-call | tf_op jit(solution)/shard_map/pallas_call | solution.py:470
  24.2 0.0 all-to-all-done
  24.2 0.0 copy-start
  24.2 0.6 %copy-done = f32[32,1,128]{2,1,0:T(1,128)} copy-done((f32[32,1,128]{2,1,0:T(1,128)}, f32[32,1,128]{2,1,0:T(1,128)S(1)}, u32[]{:S(2)}) %copy-start) | copy-done | bytes 16408
  24.8 4.6 %shard_map.111 = f32[64,128]{1,0:T(8,128)} custom-call(f32[32,128]{1,0:T(8,128)} %bitcast.21, s32[146,316]{1,0:T(8,128)} %bitcast.17, f32[49,49,316]{2,1,0:T(8,128)} %bitcast.15, f32[144,49]{1,0:T(8,128)} %get-tuple-element.11.far_hbm, f32[64,128]{1,0:T(8,128)} %get-tuple-element.12.partial_hbm, f32[392,49]{1,0:T(8,128)} %bitcast.20, f32[49,64]{1,0:T(8,128)} %bitcast.22), custom_call_target="tpu_custom_call" | custom-call | tf_op jit(solution)/shard_map/pallas_call | solution.py:522
Async XLA Ops:
  3.6 10.0 %collective-permute-start.1 = (f32[64,128]{1,0:T(8,128)}, f32[64,128]{1,0:T(8,128)S(1)}, u32[]{:S(2)}, u32[]{:S(2)}) collective-permute-start(f32[64,128]{1,0:T(8,128)} %get-tuple-element.10.source_hbm), channel_id=1, source_target_pairs={{0,0},{31,31},{1,2},{2,1},{3,4},{4,3},{5,6},{6,5},{7,8},{8,7},{9,1... | collective-permute-start | bytes 98312 | tf_op jit(solution)/shard_map/ppermute | solution.py:464
  5.0 8.6 %collective-permute-start = (f32[64,128]{1,0:T(8,128)}, f32[64,128]{1,0:T(8,128)S(1)}, u32[]{:S(2)}, u32[]{:S(2)}) collective-permute-start(f32[64,128]{1,0:T(8,128)} %get-tuple-element.10.source_hbm), channel_id=1, source_target_pairs={{0,1},{1,0},{2,3},{3,2},{4,5},{5,4},{6,7},{7,6},{8,9},{9,8},{10,11... | collective-permute-start | bytes 98312 | tf_op jit(solution)/shard_map/ppermute | solution.py:463
  8.7 15.5 %all-to-all-start = ((f32[32,1,128]{2,1,0:T(1,128)}), f32[32,1,128]{2,1,0:T(1,128)S(1)}, u32[]{:S(2)}, u32[]{:S(2)}) async-start(f32[32,1,128]{2,1,0:T(1,128)} %bitcast.23), calls=%async_computation | async-start | bytes 32768 | tf_op jit(solution)/shard_map/all_to_all | solution.py:465
  13.6 0.6 %copy-start.1 = (f32[64,128]{1,0:T(8,128)}, f32[64,128]{1,0:T(8,128)S(1)}, u32[]{:S(2)}) copy-start(f32[64,128]{1,0:T(8,128)S(1)} %collective-permute-done.1.second_hbm) | copy-start | bytes 98308
  13.6 0.6 %copy-start.2 = (f32[64,128]{1,0:T(8,128)}, f32[64,128]{1,0:T(8,128)S(1)}, u32[]{:S(2)}) copy-start(f32[64,128]{1,0:T(8,128)S(1)} %collective-permute-done.first_hbm) | copy-start | bytes 98308
  24.2 0.6 %copy-start = (f32[32,1,128]{2,1,0:T(1,128)}, f32[32,1,128]{2,1,0:T(1,128)S(1)}, u32[]{:S(2)}) copy-start(f32[32,1,128]{2,1,0:T(1,128)S(1)} %all-to-all-done) | copy-start | bytes 49156

commit v3 on v2

--- a/solution.py
+++ b/solution.py
@@ -6,7 +6,6 @@
 from jax.sharding import PartitionSpec as P
 
 AXES = ("group", "owner")
-HIGH = lax.Precision.HIGHEST
 LANES = 128
 GROUP = 8
 VMEM = pl.BlockSpec(memory_space=pltpu.VMEM)
@@ -33,12 +32,6 @@
     )
 
 
-def exact_dot(lhs, rhs, dims):
-    return lax.dot_general(
-        lhs, rhs, dims, precision=HIGH, preferred_element_type=jnp.float32
-    )
-
-
 def fast_dot(lhs, rhs, dims):
     return lax.dot_general(lhs, rhs, dims, preferred_element_type=jnp.float32)
 
@@ -69,6 +62,10 @@
         )
         total = part if total is None else total + part
     return total
+
+
+def exact_dot(lhs, rhs, dims):
+    return split_dot(halves(lhs), halves(rhs), dims)
 
 
 def source_kernel(field_ref, contrast_ref, map_ref, up_ref, source_ref, tops_ref, low, mid):
@@ -128,6 +125,8 @@
     picked_b,
     matrices_a,
     matrices_b,
+    picked_c,
+    matrices_c,
     spread,
     total,
     steps,
@@ -166,7 +165,7 @@
     mid_lanes[...] = jnp.zeros(mid_lanes.shape, jnp.int32)
     lane = lax.broadcasted_iota(jnp.int32, source_ref.shape, 1)
     from_first = (lane // half) == odd_ref[0]
-    for move in moves[0:4]:
+    for move in moves[0:9]:
         move.wait()
     rim[...] = jnp.where(from_first, first_ref[...], second_ref[...])
 
@@ -178,7 +177,6 @@
     low_rim[0:terms, :] = -rim_levels
     low_rows[0:leaves, :] = own_low.T
     low_rows[leaves : 2 * leaves, :] = rim_low.T
-    moves[4].wait()
     mid[...] = parents_of(low_rows, 2 * mids, up_mat)
     mid_levels, mid_step = levels_of(mid[...].T)
     mid_lanes[0:terms, 0 : 2 * mids] = mid_levels
@@ -187,7 +185,6 @@
     steps[1:2, :] = -rim_step
     steps[2:3, 0 : 2 * mids] = mid_step
 
-    moves[5].wait()
     near_lane = lax.broadcasted_iota(jnp.int32, (8, leaves), 1)
     for i in range(tiles):
         width = min(LANES, slots - i * LANES)
@@ -214,8 +211,6 @@
                 step = jnp.where(kinds == 1, step, 0.0)
             scale_at[i, part, :] = step
 
-    for move in moves[6:9]:
-        move.wait()
     def near_step(k, total):
         entry = jnp.broadcast_to(near_lists[pl.ds(k, 1), :], (8, leaves))
         at = near_lane + entry - half
@@ -233,9 +228,10 @@
         picked = halves(jnp.concatenate(rows, axis=0))
         return total + split_dot(halves(near_mats[k]), picked, NN)
 
-    partial_ref[...] = lax.fori_loop(
-        0, near_lists.shape[0], near_step, incident[...], unroll=9
-    )
+    near = incident[...]
+    for k in range(near_lists.shape[0]):
+        near = near_step(k, near)
+    partial_ref[...] = near
 
     moves[9].wait()
     padding = jnp.zeros((terms, wide - slots), jnp.float32)
@@ -286,6 +282,9 @@
     whole = terms // GROUP
     rounds = (whole - 1) // 2
     fill_block(0, picked_a, matrices_a)
+    for t in range(whole * GROUP, terms):
+        fill(t, 1, far_mats[:, t, :][None], picked_c, matrices_c)
+        add(1, picked_c, matrices_c)
 
     def two_blocks(i, carry):
         fill_block(2 * i + 1, picked_b, matrices_b)
@@ -300,9 +299,6 @@
         fill_block(g, *buffers[g % 2])
         add(GROUP, *buffers[(g - 1) % 2])
     add(GROUP, *buffers[(whole - 1) % 2])
-    for t in range(whole * GROUP, terms):
-        fill(t, 1, far_mats[:, t, :][None], *buffers[whole % 2])
-        add(1, *buffers[whole % 2])
     sums = total[0:targets, :] + total[targets : 2 * targets, :]
     far_ref[...] = sums[:, 0:terms] + sums[:, 64 : 64 + terms]
 
@@ -391,18 +387,16 @@
             columns.append(value)
         picked.append(jnp.concatenate(columns, axis=1)[0:terms, 0:slots])
 
-    def top_step(s):
-        matrix = far_mats_ref[s]
-        for j in range(count):
-            sums[j, pl.ds(s, 1), :] = jnp.sum(matrix * picked[j], axis=0, keepdims=True)
-
     for i in range(blocks):
         moves[2 + i].wait()
         for s in range(i * deep, (i + 1) * deep):
-            top_step(s)
+            matrix = far_mats_ref[s]
+            for j in range(count):
+                sums[j, s : s + 1, :] = jnp.sum(matrix * picked[j], axis=0, keepdims=True)
     for move in moves[2 + blocks :]:
         move.wait()
     ones = jnp.ones((8, slots), jnp.float32)
+    tops[...] = jnp.zeros(tops.shape, jnp.float32)
     for j in range(count):
         tops[pl.ds(j, 1), :] = exact_dot(ones, sums[j], NT)[0:1]
     top_rows = tops[...]
@@ -498,6 +492,8 @@
             pltpu.VMEM((GROUP * wide // LANES, 2 * targets, LANES), jnp.bfloat16),
             pltpu.VMEM((GROUP * wide // LANES, 128, LANES), jnp.bfloat16),
             pltpu.VMEM((GROUP * wide // LANES, 128, LANES), jnp.bfloat16),
+            pltpu.VMEM((wide // LANES, 2 * targets, LANES), jnp.bfloat16),
+            pltpu.VMEM((wide // LANES, 128, LANES), jnp.bfloat16),
             pltpu.VMEM((3 * GROUP, 16, LANES), jnp.int16),
             pltpu.VMEM((2 * targets, LANES), f32),
             pltpu.VMEM((8, LANES), f32),
@@ -539,6 +535,7 @@
             pltpu.VMEM((mids, terms), f32),
             pltpu.VMEM((leaves, terms), f32),
         ],
+        compiler_params=pltpu.CompilerParams(vmem_limit_bytes=55200 << 10),
     )(every_top, far_rows, far_cube, far_sums, partial, down_rows, local_map.T)
 
 

time: 29.7 us -> 27.5 us (0.926)
  Pallas kernels: 18.2 us -> 16.6 us
  local copies, waits for them, and re-layouts: 1.19 us -> 0.61 us
    pallas_call x1, Pallas kernels: 3.57 us -> 2.91 us  [body(): pl.pallas_call(source_kernel, out_shape=(jax.ShapeDtypeStruct((cells, lea...]
    unnamed x6 -> x4, local copies, waits for them, and re-layouts: 1.19 us -> 0.61 us
    pallas_call x1, Pallas kernels: 9.95 us -> 9.45 us  [body(): pl.pallas_call(local_kernel, out_shape=(jax.ShapeDtypeStruct((cells, leav...]
    pallas_call x1, Pallas kernels: 4.65 us -> 4.23 us  [body(): pl.pallas_call(final_kernel, out_shape=jax.ShapeDtypeStruct((cells, leave...]
  transfers between devices with their start and end apart: 3 -> 3, of which waited for: 0 -> 0; matrix products, arithmetic and copies ran while one was open for 0% -> 0% of each run, Pallas kernels for 34% -> 35%
where the time goes in v3:
time: 27.5 us; the launch traced here: 27.3 us
  Pallas kernels  16.6 us (60%)
  starting transfers between devices  9.97 us (36%)
  local copies, waits for them, and re-layouts  0.61 us (2%)
    pallas_call x1, Pallas kernels, body(): pl.pallas_call(local_kernel, out_shape=(jax.ShapeDtypeStruct((cells, leav...  9.45 us
    all_to_all x1, starting transfers between devices, body(): lax.all_to_all(own_tops, AXES, split_axis=0, concat_axis=0, tiled=True)  4.84 us
    pallas_call x1, Pallas kernels, body(): pl.pallas_call(final_kernel, out_shape=jax.ShapeDtypeStruct((cells, leave...  4.23 us
    ppermute x1, starting transfers between devices, body(): first = lax.ppermute(source, AXES, pairs)  3.73 us
    pallas_call x1, Pallas kernels, body(): pl.pallas_call(source_kernel, out_shape=(jax.ShapeDtypeStruct((cells, lea...  2.91 us
    ppermute x1, starting transfers between devices, body(): second = lax.ppermute(source, AXES, shifted)  1.41 us
    unnamed x4, local copies, waits for them, and re-layouts  0.61 us
  transfers between devices with their start and end apart: 3, of which 0 were waited for; matrix products, arithmetic and copies ran while one was open for 0% of the time, Pallas kernels for 35%

profile of v3, /device:TPU:0, one launch (start us, length us, event | category | flops | bytes accessed | tf_op | source)
XLA Modules:
  0.0 27.3 jit_solution(16098230974608339455)
XLA Ops:
  0.0 2.9 %shard_map.109 = (f32[64,128]{1,0:T(8,128)}, f32[32,128]{1,0:T(8,128)}) custom-call(f32[64,128]{1,0:T(8,128)} %field_ref.1, f32[64,128]{1,0:T(8,128)} %contrast_ref.1, f32[49,64]{1,0:T(8,128)} %map_hbm.1, f32[392,49]{1,0:T(8,128)} %bitcast.19), custom_call_target="tpu_custom_call" | custom-call | tf_op jit(solution)/shard_map/pallas_call | solution.py:442
  2.9 1.4 %collective-permute-start.1 = (f32[64,128]{1,0:T(8,128)}, f32[64,128]{1,0:T(8,128)S(1)}, u32[]{:S(2)}, u32[]{:S(2)}) collective-permute-start(f32[64,128]{1,0:T(8,128)} %get-tuple-element.10.source_hbm), channel_id=1, source_target_pairs={{0,0},{31,31},{1,2},{2,1},{3,4},{4,3},{5,6},{6,5},{7,8},{8,7},{9,1... | collective-permute-start | bytes 98312 | tf_op jit(solution)/shard_map/ppermute | solution.py:458
  4.3 3.7 %collective-permute-start = (f32[64,128]{1,0:T(8,128)}, f32[64,128]{1,0:T(8,128)S(1)}, u32[]{:S(2)}, u32[]{:S(2)}) collective-permute-start(f32[64,128]{1,0:T(8,128)} %get-tuple-element.10.source_hbm), channel_id=1, source_target_pairs={{0,1},{1,0},{2,3},{3,2},{4,5},{5,4},{6,7},{7,6},{8,9},{9,8},{10,11... | collective-permute-start | bytes 98312 | tf_op jit(solution)/shard_map/ppermute | solution.py:457
  8.1 4.8 %all-to-all-start = ((f32[32,1,128]{2,1,0:T(1,128)}), f32[32,1,128]{2,1,0:T(1,128)S(1)}, u32[]{:S(2)}, u32[]{:S(2)}) async-start(f32[32,1,128]{2,1,0:T(1,128)} %bitcast.23), calls=%async_computation | async-start | bytes 32768 | tf_op jit(solution)/shard_map/all_to_all | solution.py:459
  12.9 0.0 collective-permute-done.1.second_hbm
  12.9 0.0 copy-start
  12.9 0.0 collective-permute-done.first_hbm
  12.9 0.0 copy-start.1
  12.9 0.6 %copy-done = f32[64,128]{1,0:T(8,128)} copy-done((f32[64,128]{1,0:T(8,128)}, f32[64,128]{1,0:T(8,128)S(1)}, u32[]{:S(2)}) %copy-start) | copy-done | bytes 32792
  13.5 0.0 copy-done.1
  13.6 9.5 %shard_map.110 = (f32[64,128]{1,0:T(8,128)}, f32[144,49]{1,0:T(8,128)}) custom-call(s32[1]{0:T(128)} %bitcast.7.odd_ref, f32[64,128]{1,0:T(8,128)} %get-tuple-element.10.source_hbm, f32[64,128]{1,0:T(8,128)} %copy-done.1, f32[64,128]{1,0:T(8,128)} %copy-done, f32[64,128]{1,0:T(8,128)} %incident_hbm.1, s32[27,128]{1,0:T(8,128)} %near_lists_hbm.1, ...), custom_call_target="tpu_custom_call" | custom-call | tf_op jit(solution)/shard_map/pallas_call | solution.py:464
  23.0 0.0 all-to-all-done
  23.0 4.2 %shard_map.111 = f32[64,128]{1,0:T(8,128)} custom-call(f32[32,128]{1,0:T(8,128)S(1)} %bitcast.14, s32[146,316]{1,0:T(8,128)} %bitcast.18, f32[49,49,316]{2,1,0:T(8,128)} %bitcast.16, f32[144,49]{1,0:T(8,128)} %get-tuple-element.11.far_hbm, f32[64,128]{1,0:T(8,128)} %get-tuple-element.12.partial_hbm, f32[392,49]{1,0:T(8,128)} %bitcast.21, f32[49,64]{1,0:T(8,128)} %bitcast.22), custom_call_target="tpu_custom_call" | custom-call | tf_op jit(solution)/shard_map/pallas_call | solution.py:518
Async XLA Ops:
  2.9 10.0 %collective-permute-start.1 = (f32[64,128]{1,0:T(8,128)}, f32[64,128]{1,0:T(8,128)S(1)}, u32[]{:S(2)}, u32[]{:S(2)}) collective-permute-start(f32[64,128]{1,0:T(8,128)} %get-tuple-element.10.source_hbm), channel_id=1, source_target_pairs={{0,0},{31,31},{1,2},{2,1},{3,4},{4,3},{5,6},{6,5},{7,8},{8,7},{9,1... | collective-permute-start | bytes 98312 | tf_op jit(solution)/shard_map/ppermute | solution.py:458
  4.3 8.6 %collective-permute-start = (f32[64,128]{1,0:T(8,128)}, f32[64,128]{1,0:T(8,128)S(1)}, u32[]{:S(2)}, u32[]{:S(2)}) collective-permute-start(f32[64,128]{1,0:T(8,128)} %get-tuple-element.10.source_hbm), channel_id=1, source_target_pairs={{0,1},{1,0},{2,3},{3,2},{4,5},{5,4},{6,7},{7,6},{8,9},{9,8},{10,11... | collective-permute-start | bytes 98312 | tf_op jit(solution)/shard_map/ppermute | solution.py:457
  8.1 15.0 %all-to-all-start = ((f32[32,1,128]{2,1,0:T(1,128)}), f32[32,1,128]{2,1,0:T(1,128)S(1)}, u32[]{:S(2)}, u32[]{:S(2)}) async-start(f32[32,1,128]{2,1,0:T(1,128)} %bitcast.23), calls=%async_computation | async-start | bytes 32768 | tf_op jit(solution)/shard_map/all_to_all | solution.py:459
  12.9 0.6 %copy-start = (f32[64,128]{1,0:T(8,128)}, f32[64,128]{1,0:T(8,128)S(1)}, u32[]{:S(2)}) copy-start(f32[64,128]{1,0:T(8,128)S(1)} %collective-permute-done.1.second_hbm) | copy-start | bytes 98308
  12.9 0.6 %copy-start.1 = (f32[64,128]{1,0:T(8,128)}, f32[64,128]{1,0:T(8,128)S(1)}, u32[]{:S(2)}) copy-start(f32[64,128]{1,0:T(8,128)S(1)} %collective-permute-done.first_hbm) | copy-start | bytes 98308
